TPU v7x, 32 devices: a whole 2x2x4 slice. The times are simulated.
32 devices in a mesh: dp: 4 (over y, x), tr: 2 (over core), tc: 4 (over z).
Axes of the slice: x: 2, y: 2, z: 4, core: 2. Of those that a mesh axis runs over, the one named last changes fastest.
Arguments:
- activations: bfloat16 [4096, 3072], P(('dp', 'tc'), 'tr'), may hold values from -6 to 6
- cotangent: bfloat16 [4096, 8192], P(('dp', 'tr'), 'tc'), may hold values from -0.09375 to 0.09375
- master: float32 [2, 1536, 8192], P('tr', ('dp', 'tc')), may hold values from -3 to 3
- moment: float32 [2, 1536, 8192], P('tr', ('dp', 'tc')), may hold values from -2 to 2
- second: float32 [2, 1536, 8192], P('tr', ('dp', 'tc')), may hold values from 0.05 to 2
Outputs:
- new_master: float32 [2, 1536, 8192], P('tr', ('dp', 'tc'))
- new_moment: float32 [2, 1536, 8192], P('tr', ('dp', 'tc'))
- new_second: float32 [2, 1536, 8192], P('tr', ('dp', 'tc'))
All inputs are finite; a program needn't handle non-finite values.
Results may differ from a plain program's by a relative error of at most 0.0003.
Values may be sent and summed in bfloat16 or wider, within the bound.
A program may use at most 128 MiB of HBM per device.

v0:
```python
import jax
import jax.numpy as jnp
from jax import lax
from jax.sharding import PartitionSpec as P

first_decay = 0.9
second_decay = 0.95
learn_rate = 0.0003
weight_decay = 0.1
epsilon = 1e-08
first_fix = 1.0 - 0.9**10
second_fix = 1.0 - 0.95**10


def shards(activations, cotangent, master, moment, second):
    act_rows = lax.all_gather(activations, "tc", axis=0, tiled=True)
    cot_rows = lax.all_gather(cotangent, "tr", axis=0, tiled=True)
    replicas = lax.axis_size("dp")
    columns = lax.axis_size("tc")
    feature_count = act_rows.shape[1]
    unit_count = cot_rows.shape[1]
    owned = feature_count // (replicas * columns)
    summed = lax.psum_scatter(
        lax.dot_general(
            act_rows, cot_rows, (((0,), (0,)), ((), ())), preferred_element_type=jnp.float32
        ),
        "dp",
        scatter_dimension=0,
        tiled=True,
    )
    summed = summed.reshape(columns, owned, unit_count)
    grad = lax.all_to_all(summed, "tc", split_axis=0, concat_axis=2, tiled=True)
    new_moment = first_decay * moment + (1.0 - first_decay) * grad
    new_second = second_decay * second + (1.0 - second_decay) * grad * grad
    update = new_moment / first_fix / (jnp.sqrt(new_second / second_fix) + epsilon)
    new_master = master - learn_rate * (update + weight_decay * master)
    return (new_master, new_moment, new_second)


def solution(mesh):
    return jax.shard_map(
        shards,
        mesh=mesh,
        in_specs=(
            P(("dp", "tc"), "tr"),
            P(("dp", "tr"), "tc"),
            P("tr", ("dp", "tc"), None),
            P("tr", ("dp", "tc"), None),
            P("tr", ("dp", "tc"), None),
        ),
        out_specs=(
            P("tr", ("dp", "tc"), None),
            P("tr", ("dp", "tc"), None),
            P("tr", ("dp", "tc"), None),
        ),
        check_vma=False,
    )
```

profile of v0, /device:TPU:0, one launch (start us, length us, event | category | flops | bytes accessed | tf_op | source)
XLA Modules:
  0.0 313.0 jit_solution(5629304341752762359)
XLA Ops:
  7.2 0.0 all-gather.5.cloned.1.call-start
  7.2 0.7 all-gather.5.cloned.1.call-update
  7.9 0.0 all-gather.3.cloned.1.call-start
  7.9 0.7 all-gather.3.cloned.1.call-update
  8.6 0.0 reduce-scatter.2.cloned.1.call-start
  8.7 17.2 %all-gather.5.cloned.1.call-done = bf16[1024,2048]{1,0:T(8,128)(2,1)} async-done(((bf16[512,2048]{1,0:T(8,128)(2,1)}), bf16[1024,2048]{1,0:T(8,128)(2,1)}) %all-gather.5.cloned.1.call-update) | async-done | bytes 4194320 | tf_op jit(solution)/shard_map/all_gather | solution.py:17
  25.9 66.2 %all-gather.3.cloned.1.call-done = bf16[1024,1536]{1,0:T(8,128)(2,1)} async-done(((bf16[256,1536]{1,0:T(8,128)(2,1)}), bf16[1024,1536]{1,0:T(8,128)(2,1)}) %all-gather.3.cloned.1.call-update) | async-done | bytes 3145744 | tf_op jit(solution)/shard_map/all_gather | solution.py:16
  92.2 12.3 %fusion.2 = f32[1536,2048]{1,0:T(8,128)} fusion(bf16[1024,1536]{1,0:T(8,128)(2,1)} %all-gather.3.cloned.1.call-done, bf16[1024,2048]{1,0:T(8,128)(2,1)} %all-gather.5.cloned.1.call-done), kind=kOutput, calls=%fused_computation.4 | convolution fusion | flops 6442450944 | bytes 19922944 | tf_op jit(solution)/shard_map/dot_general | solution.py:24
  104.4 0.0 reduce-scatter.2.cloned.1.call-update
  104.4 119.4 %reduce-scatter.2.cloned.1.call-done = f32[384,2048]{1,0:T(8,128)} async-done(((f32[1536,2048]{1,0:T(8,128)}), f32[384,2048]{1,0:T(8,128)}) %reduce-scatter.2.cloned.1.call-update) | async-done | bytes 3145744 | tf_op jit(solution)/shard_map/reduce_scatter | solution.py:23
  223.8 0.0 copy-start.2
  223.8 75.3 %all_to_all.18 = f32[4,96,2048]{2,1,0:T(8,128)S(1)} all-to-all(f32[4,96,2048]{2,1,0:T(8,128)} %bitcast.10), channel_id=1, replica_groups=mesh['dp'=4,'tr'=2,'tc'=4] {'tc'}, dimensions={0} | all-to-all | bytes 6291456 | tf_op jit(solution)/shard_map/all_to_all | solution.py:32
  299.2 0.0 copy-start
  299.2 0.0 copy-start.1
  299.2 0.2 copy.9
  299.4 0.0 copy-done.2
  299.4 1.7 copy-done
  301.1 1.0 copy-done.1
  302.0 4.4 %multiply_subtract_fusion = (f32[1,96,8192]{2,1,0:T(8,128)}, f32[1,96,8192]{2,1,0:T(8,128)}, f32[1,96,8192]{2,1,0:T(8,128)}) fusion(f32[1,96,8192]{2,1,0:T(8,128)S(1)} %copy-done, f32[1,96,8192]{2,1,0:T(8,128)S(1)} %bitcast.9, f32[1,96,8192]{2,1,0:T(8,128)S(1)} %copy-done.1, f32[1,96,8192]{2,1,0:T(8,128)S(1)} %copy-done.2), kind=kLoop, calls=%fused_computation.2 | loop fusion | flops 11796480 | bytes 22020096 | tf_op jit(solution)/shard_map/sub | solution.py:36
Async XLA Ops:
  7.2 18.8 %all-gather.5.cloned.1.call-start = ((), (), s32[]{:S(2)}) async-start(), calls=%async_computation.3 | async-start | bytes 6291456 | tf_op jit(solution)/shard_map/all_gather | solution.py:17
  7.9 84.3 %all-gather.3.cloned.1.call-start = ((), (), s32[]{:S(2)}) async-start(), calls=%async_computation.2 | async-start | bytes 3932160 | tf_op jit(solution)/shard_map/all_gather | solution.py:16
  8.6 215.2 %reduce-scatter.2.cloned.1.call-start = ((), (), s32[]{:S(2)}) async-start(), calls=%async_computation.4 | async-start | bytes 15728640 | tf_op jit(solution)/shard_map/reduce_scatter | solution.py:23
  223.8 75.6 %copy-start.2 = (f32[1,96,8192]{2,1,0:T(8,128)S(1)}, f32[1,96,8192]{2,1,0:T(8,128)}, u32[]{:S(2)}) copy-start(f32[1,96,8192]{2,1,0:T(8,128)} %param.9) | copy-start | bytes 9437188
  299.2 1.9 copy-start
  299.2 2.8 copy-start.1
Sparse Core Ops, SparseCore 0:
  9.5 16.3 all-gather.4
  27.5 64.6 all-gather.2
  104.6 119.2 reduce-scatter.1
where the time goes:
time: 313 us
  waiting for transfers between devices  204 us (65%)
  blocking collectives  75.3 us (24%)
  between operations  13.8 us (4%)
  matrix products  12.3 us (4%)
  other arithmetic  4.43 us (1%)
    reduce_scatter x1, waiting for transfers between devices, shards(): lax.psum_scatter(lax.dot_general(act_rows, cot_rows, (((0,), (0,)), ((),...  119 us
    all_to_all x1, blocking collectives, shards(): grad = lax.all_to_all(summed, 'tc', split_axis=0, concat_axis=2, tiled=True)  75.3 us
    all_gather x1, waiting for transfers between devices, shards(): act_rows = lax.all_gather(activations, 'tc', axis=0, tiled=True)  66.2 us
    all_gather x1, waiting for transfers between devices, shards(): cot_rows = lax.all_gather(cotangent, 'tr', axis=0, tiled=True)  17.2 us
    dot_general x1, matrix products, shards(): lax.dot_general(act_rows, cot_rows, (((0,), (0,)), ((), ())), preferred_e...  12.3 us
  transfers between devices with their start and end apart: 3, of which 3 were waited for; matrix products, arithmetic and copies ran while one was open for 0% of the time, Pallas kernels for 0%

commit v1 on v0

--- a/solution.py
+++ b/solution.py
@@ -1,6 +1,10 @@
+import functools
+
 import jax
 import jax.numpy as jnp
 from jax import lax
+from jax.experimental import pallas as pl
+from jax.experimental.pallas import tpu as pltpu
 from jax.sharding import PartitionSpec as P
 
 first_decay = 0.9
@@ -11,8 +15,251 @@
 first_fix = 1.0 - 0.9**10
 second_fix = 1.0 - 0.95**10
 
-
-def shards(activations, cotangent, master, moment, second):
+MESH = pl.DeviceIdType.MESH
+VMEM_BYTES = 60 * 2**20
+CHUNKS = 4
+SCALE = 1.0
+WIRE = jnp.float32
+
+
+def grad_kernel(sizes, act, cot, out, abuf, cbuf, at, obuf, ld_sem, adp_s, adp_r, az_s, az_r, c_s, c_r, o_s, o_r):
+    dp, tr, tc, chunks, tile = sizes
+    r, c, z = lax.axis_index("dp"), lax.axis_index("tr"), lax.axis_index("tc")
+    rx = r + 1 - 2 * lax.rem(r, 2)
+    ry = lax.rem(r + 2, 4)
+    rd = 3 - r
+    rel = (r, rx, ry, rd)
+    atok, rows = abuf.shape[2], abuf.shape[3]
+    ctok, nu = cbuf.shape[3], cbuf.shape[4]
+    units = chunks * nu
+    half = ctok // 2
+
+    barrier = pltpu.get_barrier_semaphore()
+    peers = [{"dp": q} for q in (rx, ry, rd)] + [{"tr": 1 - c}]
+    peers += [{"tc": lax.rem(z + j, tc)} for j in range(1, tc)]
+    for peer in peers:
+        pl.semaphore_signal(barrier, inc=1, device_id=peer, device_id_type=MESH)
+    pl.semaphore_wait(barrier, len(peers))
+
+    def remote(src, dst, s, d, peer):
+        return pltpu.make_async_remote_copy(
+            src_ref=src, dst_ref=dst, send_sem=s, recv_sem=d, device_id=peer, device_id_type=MESH
+        )
+
+    def act_cols(q):
+        return act.at[:, pl.ds(pl.multiple_of(q * rows, 128), rows)]
+
+    def a_dp(k):
+        return remote(act_cols(rel[k]), abuf.at[r, z], adp_s.at[k], adp_r.at[k], {"dp": rel[k]})
+
+    def a_z(d, s, k):
+        block = z - s if d == 0 else z + s
+        to = z + 1 if d == 0 else z - 1
+        slot = abuf.at[rel[k], block]
+        src = act_cols(r) if s == 0 and k == 0 else slot
+        return remote(src, slot, az_s.at[d, s, k], az_r.at[d, s, k], {"tc": to})
+
+    def a_z_sends(d, s):
+        return (z >= s) & (z < tc - 1) if d == 0 else (z < tc - s) & (z > 0)
+
+    def a_z_gets(d, s):
+        return z >= s + 1 if d == 0 else z < tc - 1 - s
+
+    def send_z(s, k):
+        for d in range(2):
+            @pl.when(a_z_sends(d, s))
+            def _():
+                a_z(d, s, k).start()
+
+    def got_z(s, k):
+        for d in range(2):
+            @pl.when(a_z_gets(d, s))
+            def _():
+                a_z(d, s, k).wait_recv()
+
+    def cot_cols(u):
+        return cot.at[:, pl.ds(u * nu, nu)]
+
+    def c_copy(flow, u):
+        if flow == 0:
+            return remote(cot_cols(u), cbuf.at[u, r, c], c_s.at[0, u], c_r.at[0, u], {"dp": rx})
+        if flow == 1:
+            return remote(cot_cols(u), cbuf.at[u, r, c], c_s.at[1, u], c_r.at[1, u], {"dp": ry})
+        if flow == 2:
+            part = cbuf.at[u, ry, c, pl.ds(0, half)]
+            return remote(part, part, c_s.at[2, u], c_r.at[2, u], {"dp": rx})
+        if flow == 3:
+            part = cbuf.at[u, rx, c, pl.ds(half, half)]
+            return remote(part, part, c_s.at[3, u], c_r.at[3, u], {"dp": ry})
+        k = flow - 4
+        slot = cbuf.at[u, rel[k], c]
+        src = cot_cols(u) if k == 0 else slot
+        return remote(src, slot, c_s.at[flow, u], c_r.at[flow, u], {"tr": 1 - c})
+
+    def own(u):
+        for flow in (0, 1, 4):
+            c_copy(flow, u).start()
+
+    def got_xy(u):
+        c_copy(0, u).wait_recv()
+        c_copy(3, u).start()
+        c_copy(5, u).start()
+        c_copy(1, u).wait_recv()
+        c_copy(2, u).start()
+        c_copy(6, u).start()
+
+    def got_diag(u):
+        c_copy(2, u).wait_recv()
+        c_copy(3, u).wait_recv()
+        c_copy(7, u).start()
+
+    def local_c(u):
+        return pltpu.make_async_copy(cot_cols(u), cbuf.at[u, r, c], ld_sem.at[1 + u])
+
+    local_a = pltpu.make_async_copy(act_cols(r), abuf.at[r, z], ld_sem.at[0])
+
+    def o_copy(j, u):
+        to = lax.rem(z + j, tc)
+        dst = out.at[:, pl.ds(pl.multiple_of(z * units + u * nu, 128), nu)]
+        if j == 0:
+            return pltpu.make_async_copy(obuf.at[u, z], dst, o_s.at[0, u])
+        return remote(obuf.at[u, to], dst, o_s.at[j, u], o_r.at[j, u], {"tc": to})
+
+    owned = rows // tc
+
+    def compute(u):
+        for flow in range(4, 8):
+            c_copy(flow, u).wait_recv()
+        local_c(u).wait()
+
+        @pl.loop(0, nu // tile)
+        def _(t):
+            cols = pl.ds(pl.multiple_of(t * tile, tile), tile)
+            total = jnp.zeros((rows, tile), jnp.float32)
+            for q in range(dp):
+                rhs = cbuf[u, q, :, :, cols].reshape(tr * ctok, tile)
+                total += jnp.dot(at[q], rhs, preferred_element_type=jnp.float32)
+            total = (total * SCALE).astype(WIRE)
+            for j in range(tc):
+                obuf[u, j, :, cols] = total[j * owned:(j + 1) * owned]
+
+        for j in (*range(1, tc), 0):
+            o_copy(j, u).start()
+
+    for k in range(1, 4):
+        a_dp(k).start()
+    send_z(0, 0)
+    own(0)
+    own(1)
+    local_a.start()
+    for u in range(chunks):
+        local_c(u).start()
+    for k in range(1, 4):
+        a_dp(k).wait_recv()
+        send_z(0, k)
+
+    def forward(s, k):
+        got_z(s - 1, k)
+        send_z(s, k)
+
+    def step_xy(u):
+        got_xy(u)
+        if u + 2 < chunks:
+            own(u + 2)
+
+    def last_a(k):
+        got_z(tc - 2, k)
+        if k == 0:
+            local_a.wait()
+        at[rel[k]] = abuf[rel[k]].reshape(tc * atok, rows).T
+
+    moves = [(forward, s, k) for s in range(1, tc - 1) for k in range(4)]
+    moves += [(last_a, k) for k in range(4)]
+    turns = []
+    for u in range(chunks):
+        turns.append((step_xy, u))
+        if u >= 1:
+            turns.append((got_diag, u - 1))
+    order = []
+    early = 2 * (chunks // 2)
+    for i, move in enumerate(moves):
+        order.append(move)
+        if i >= 2 and turns and (i - 2) % (len(moves) // early) == 0 and len(turns) > chunks // 2:
+            order.append(turns.pop(0))
+    for f, *args in order:
+        f(*args)
+    done = 0
+    for f, u in turns:
+        f(u)
+        if f is got_diag:
+            while done <= u:
+                compute(done)
+                done += 1
+    got_diag(chunks - 1)
+    while done < chunks:
+        compute(done)
+        done += 1
+
+    for k in range(1, 4):
+        a_dp(k).wait_send()
+    for d in range(2):
+        for s in range(tc - 1):
+            @pl.when(a_z_sends(d, s))
+            def _():
+                for k in range(4):
+                    a_z(d, s, k).wait_send()
+    for u in range(chunks):
+        for flow in range(8):
+            c_copy(flow, u).wait_send()
+    for u in range(chunks):
+        o_copy(0, u).wait()
+        for j in range(1, tc):
+            o_copy(j, u).wait_send()
+            o_copy(j, u).wait_recv()
+
+
+def vmem_plan(activations, cotangent, dp, tr, tc):
+    atok, features = activations.shape
+    ctok, units = cotangent.shape
+    rows = features // dp
+    return dp * tc * atok * rows * 4 + dp * tr * ctok * units * 2 + rows * units * 2
+
+
+def gathered(activations, cotangent, dp, tr, tc):
+    atok, features = activations.shape
+    ctok, units = cotangent.shape
+    rows = features // dp
+    owned = rows // tc
+    chunks = CHUNKS
+    nu = units // chunks
+    tile = min(nu, 256)
+    return pl.pallas_call(
+        functools.partial(grad_kernel, (dp, tr, tc, chunks, tile)),
+        out_shape=jax.ShapeDtypeStruct((owned, tc * units), WIRE),
+        in_specs=[pl.BlockSpec(memory_space=pl.ANY)] * 2,
+        out_specs=pl.BlockSpec(memory_space=pl.ANY),
+        scratch_shapes=[
+            pltpu.VMEM((dp, tc, atok, rows), jnp.bfloat16),
+            pltpu.VMEM((chunks, dp, tr, ctok, nu), jnp.bfloat16),
+            pltpu.VMEM((dp, rows, tc * atok), jnp.bfloat16),
+            pltpu.VMEM((chunks, tc, owned, nu), WIRE),
+            pltpu.SemaphoreType.DMA((1 + chunks,)),
+            pltpu.SemaphoreType.DMA((4,)),
+            pltpu.SemaphoreType.DMA((4,)),
+            pltpu.SemaphoreType.DMA((2, tc - 1, 4)),
+            pltpu.SemaphoreType.DMA((2, tc - 1, 4)),
+            pltpu.SemaphoreType.DMA((8, chunks)),
+            pltpu.SemaphoreType.DMA((8, chunks)),
+            pltpu.SemaphoreType.DMA((tc, chunks)),
+            pltpu.SemaphoreType.DMA((tc, chunks)),
+        ],
+        compiler_params=pltpu.CompilerParams(
+            collective_id=0, has_side_effects=True, vmem_limit_bytes=VMEM_BYTES
+        ),
+    )(activations, cotangent)
+
+
+def native(activations, cotangent):
     act_rows = lax.all_gather(activations, "tc", axis=0, tiled=True)
     cot_rows = lax.all_gather(cotangent, "tr", axis=0, tiled=True)
     replicas = lax.axis_size("dp")
@@ -29,7 +276,17 @@
         tiled=True,
     )
     summed = summed.reshape(columns, owned, unit_count)
-    grad = lax.all_to_all(summed, "tc", split_axis=0, concat_axis=2, tiled=True)
+    return lax.all_to_all(summed, "tc", split_axis=0, concat_axis=2, tiled=True)
+
+
+def shards(activations, cotangent, master, moment, second):
+    dp, tr, tc = (lax.axis_size(name) for name in ("dp", "tr", "tc"))
+    small = vmem_plan(activations, cotangent, dp, tr, tc) < VMEM_BYTES * 3 // 4
+    if dp == 4 and tr == 2 and tc > 2 and small:
+        grad = gathered(activations, cotangent, dp, tr, tc)
+        grad = (grad.astype(jnp.float32) * (1.0 / SCALE)).reshape(master.shape)
+    else:
+        grad = native(activations, cotangent)
     new_moment = first_decay * moment + (1.0 - first_decay) * grad
     new_second = second_decay * second + (1.0 - second_decay) * grad * grad
     update = new_moment / first_fix / (jnp.sqrt(new_second / second_fix) + epsilon)

time: 313 us -> 137 us (0.44)
  waiting for transfers between devices: 204 us -> 0 us
  Pallas kernels: 0 us -> 129 us
  blocking collectives: 75.3 us -> 0 us
  between operations: 13.8 us -> 0.65 us
  matrix products: 12.3 us -> 0 us
    pallas_call x0 -> x1, Pallas kernels: none -> 129 us  [gathered(): pl.pallas_call(functools.partial(grad_kernel, (dp, tr, tc, chunks, tile))...]
    reduce_scatter x1 -> x0, waiting for transfers between devices: 119 us -> none  [shards(): lax.psum_scatter(lax.dot_general(act_rows, cot_rows, (((0,), (0,)), ((),...]
    all_gather x2 -> x0, waiting for transfers between devices: 83.5 us -> none  [the longest x1 66.2 us: shards(): act_rows = lax.all_gather(activations, 'tc', axis=0, tiled=True)]
    all_to_all x1 -> x0, blocking collectives: 75.3 us -> none  [shards(): grad = lax.all_to_all(summed, 'tc', split_axis=0, concat_axis=2, tiled=True)]
    dot_general x1 -> x0, matrix products: 12.3 us -> none  [shards(): lax.dot_general(act_rows, cot_rows, (((0,), (0,)), ((), ())), preferred_e...]
  transfers between devices with their start and end apart: 3 -> 0, of which waited for: 3 -> 0; matrix products, arithmetic and copies ran while one was open for 0% -> 0% of each run, Pallas kernels for 0% -> 0%
where the time goes in v1:
time: 137 us; the launch traced here: 136 us
  Pallas kernels  129 us (94%)
  other arithmetic  6.92 us (5%)
    pallas_call x1, Pallas kernels, gathered(): pl.pallas_call(functools.partial(grad_kernel, (dp, tr, tc, chunks, tile))...  129 us
    sub x1, other arithmetic, shards(): new_master = master - learn_rate * (update + weight_decay * master)  6.92 us

profile of v1, /device:TPU:0, one launch (start us, length us, event | category | flops | bytes accessed | tf_op | source)
XLA Modules:
  0.0 136.5 jit_solution(15194837168913530028)
XLA Ops:
  0.6 0.0 copy-start
  0.6 128.9 %shard_map.76 = f32[96,8192]{1,0:T(8,128)} custom-call(bf16[256,1536]{1,0:T(8,128)(2,1)} %act.1, bf16[512,2048]{1,0:T(8,128)(2,1)} %cot.1), custom_call_target="tpu_custom_call" | custom-call | tf_op jit(solution)/shard_map/pallas_call | solution.py:236
  129.5 0.0 copy-done
  129.5 6.9 %multiply_subtract_fusion = (f32[1,96,8192]{2,1,0:T(8,128)}, f32[1,96,8192]{2,1,0:T(8,128)}, f32[1,96,8192]{2,1,0:T(8,128)}) fusion(f32[1,96,8192]{2,1,0:T(8,128)S(1)} %copy-done, f32[96,8192]{1,0:T(8,128)} %shard_map.76, f32[1,96,8192]{2,1,0:T(8,128)} %param.8, f32[1,96,8192]{2,1,0:T(8,128)} %param.9), kind=kLoop, calls=%fused_computation.4 | loop fusion | flops 11796480 | bytes 22020096 | tf_op jit(solution)/shard_map/sub | solution.py:293
Async XLA Ops:
  0.6 128.9 %copy-start = (f32[1,96,8192]{2,1,0:T(8,128)S(1)}, f32[1,96,8192]{2,1,0:T(8,128)}, u32[]{:S(2)}) copy-start(f32[1,96,8192]{2,1,0:T(8,128)} %param.7) | copy-start | bytes 9437188

commit v2 on v1

--- a/solution.py
+++ b/solution.py
@@ -18,11 +18,53 @@
 MESH = pl.DeviceIdType.MESH
 VMEM_BYTES = 60 * 2**20
 CHUNKS = 4
-SCALE = 1.0
-WIRE = jnp.float32
-
-
-def grad_kernel(sizes, act, cot, out, abuf, cbuf, at, obuf, ld_sem, adp_s, adp_r, az_s, az_r, c_s, c_r, o_s, o_r):
+LEVELS = 12.0
+STEPS = 128.0 * LEVELS
+
+
+def encode(v):
+    y = jnp.abs(v) * 2.0**8
+    tiny = y < 1.0
+    y = jnp.where(tiny, y + 1.0, y)
+    high = y >= 2.0**16
+    power = jnp.where(high, 2.0**78, jnp.where(tiny, 2.0**-126, 2.0**-114))
+    y = jnp.where(high, y * 2.0**-16, y)
+    for s in (8, 4, 2, 1):
+        big = y >= 2.0**s
+        y = jnp.where(big, y * 2.0**-s, y)
+        power = jnp.where(big, power * 2.0 ** (12 * s), power)
+    step = jnp.minimum(jnp.floor((y - 1.0) * STEPS + 0.5), STEPS - 1.0)
+    quotient = jnp.floor((step + 0.5) * (1.0 / LEVELS))
+    rest = step - LEVELS * quotient
+    for s in (8, 4, 2, 1):
+        big = rest >= s
+        rest = jnp.where(big, rest - s, rest)
+        power = jnp.where(big, power * 2.0**s, power)
+    code = power * (1.0 + quotient * (1.0 / 128.0))
+    return jnp.where(v < 0.0, -code, code).astype(jnp.bfloat16)
+
+
+def decode(code):
+    code = code.astype(jnp.float32)
+    x = jnp.abs(code)
+    top, mid = x >= 2.0**66, x >= 2.0**-30
+    x = x * jnp.where(top, 2.0**-66, jnp.where(mid, 2.0**30, 2.0**126))
+    power = jnp.where(top, 2.0**15, jnp.where(mid, 2.0**7, 2.0**-1))
+    for s in (4, 2, 1):
+        big = x >= 2.0 ** (12 * s)
+        x = jnp.where(big, x * 2.0 ** (-12 * s), x)
+        power = jnp.where(big, power * 2.0**s, power)
+    rest = jnp.zeros_like(x)
+    for s in (8, 4, 2, 1):
+        big = x >= 2.0**s
+        x = jnp.where(big, x * 2.0**-s, x)
+        rest = jnp.where(big, rest + s, rest)
+    x = x + rest * (1.0 / STEPS)
+    y = jnp.where(power < 1.0, x - 1.0, x * power) * 2.0**-8
+    return jnp.where(code < 0.0, -y, y)
+
+
+def grad_kernel(sizes, act, cot, out, abuf, cbuf, at, obuf, rbuf, dbuf, ld_sem, adp_s, adp_r, az_s, az_r, c_s, c_r, o_s, o_r, st_sem):
     dp, tr, tc, chunks, tile = sizes
     r, c, z = lax.axis_index("dp"), lax.axis_index("tr"), lax.axis_index("tc")
     rx = r + 1 - 2 * lax.rem(r, 2)
@@ -120,10 +162,11 @@
 
     def o_copy(j, u):
         to = lax.rem(z + j, tc)
-        dst = out.at[:, pl.ds(pl.multiple_of(z * units + u * nu, 128), nu)]
-        if j == 0:
-            return pltpu.make_async_copy(obuf.at[u, z], dst, o_s.at[0, u])
-        return remote(obuf.at[u, to], dst, o_s.at[j, u], o_r.at[j, u], {"tc": to})
+        return remote(obuf.at[u, to], rbuf.at[u, z], o_s.at[j, u], o_r.at[j, u], {"tc": to})
+
+    def store(block, j, u):
+        dst = out.at[:, pl.ds(pl.multiple_of(block * units + u * nu, 128), nu)]
+        return pltpu.make_async_copy(dbuf.at[u, block], dst, st_sem.at[j, u])
 
     owned = rows // tc
 
@@ -139,12 +182,29 @@
             for q in range(dp):
                 rhs = cbuf[u, q, :, :, cols].reshape(tr * ctok, tile)
                 total += jnp.dot(at[q], rhs, preferred_element_type=jnp.float32)
-            total = (total * SCALE).astype(WIRE)
             for j in range(tc):
-                obuf[u, j, :, cols] = total[j * owned:(j + 1) * owned]
-
-        for j in (*range(1, tc), 0):
+                part = total[j * owned:(j + 1) * owned]
+                obuf[u, j, :, cols] = encode(part)
+
+                @pl.when(z == j)
+                def _():
+                    dbuf[u, j, :, cols] = part
+
+        for j in range(1, tc):
             o_copy(j, u).start()
+        store(z, 0, u).start()
+
+    def finish(u):
+        for j in range(1, tc):
+            o_copy(j, u).wait_recv()
+            block = lax.rem(z + tc - j, tc)
+
+            @pl.loop(0, owned // 16)
+            def _(i):
+                part = pl.ds(pl.multiple_of(i * 16, 16), 16)
+                dbuf[u, block, part] = decode(rbuf[u, block, part])
+
+            store(block, j, u).start()
 
     for k in range(1, 4):
         a_dp(k).start()
@@ -199,6 +259,8 @@
     while done < chunks:
         compute(done)
         done += 1
+    for u in range(chunks):
+        finish(u)
 
     for k in range(1, 4):
         a_dp(k).wait_send()
@@ -212,17 +274,17 @@
         for flow in range(8):
             c_copy(flow, u).wait_send()
     for u in range(chunks):
-        o_copy(0, u).wait()
+        store(z, 0, u).wait()
         for j in range(1, tc):
             o_copy(j, u).wait_send()
-            o_copy(j, u).wait_recv()
+            store(lax.rem(z + tc - j, tc), j, u).wait()
 
 
 def vmem_plan(activations, cotangent, dp, tr, tc):
     atok, features = activations.shape
     ctok, units = cotangent.shape
     rows = features // dp
-    return dp * tc * atok * rows * 4 + dp * tr * ctok * units * 2 + rows * units * 2
+    return dp * tc * atok * rows * 4 + dp * tr * ctok * units * 2 + rows * units * 8
 
 
 def gathered(activations, cotangent, dp, tr, tc):
@@ -235,14 +297,16 @@
     tile = min(nu, 256)
     return pl.pallas_call(
         functools.partial(grad_kernel, (dp, tr, tc, chunks, tile)),
-        out_shape=jax.ShapeDtypeStruct((owned, tc * units), WIRE),
+        out_shape=jax.ShapeDtypeStruct((owned, tc * units), jnp.float32),
         in_specs=[pl.BlockSpec(memory_space=pl.ANY)] * 2,
         out_specs=pl.BlockSpec(memory_space=pl.ANY),
         scratch_shapes=[
             pltpu.VMEM((dp, tc, atok, rows), jnp.bfloat16),
             pltpu.VMEM((chunks, dp, tr, ctok, nu), jnp.bfloat16),
             pltpu.VMEM((dp, rows, tc * atok), jnp.bfloat16),
-            pltpu.VMEM((chunks, tc, owned, nu), WIRE),
+            pltpu.VMEM((chunks, tc, owned, nu), jnp.bfloat16),
+            pltpu.VMEM((chunks, tc, owned, nu), jnp.bfloat16),
+            pltpu.VMEM((chunks, tc, owned, nu), jnp.float32),
             pltpu.SemaphoreType.DMA((1 + chunks,)),
             pltpu.SemaphoreType.DMA((4,)),
             pltpu.SemaphoreType.DMA((4,)),
@@ -250,6 +314,7 @@
             pltpu.SemaphoreType.DMA((2, tc - 1, 4)),
             pltpu.SemaphoreType.DMA((8, chunks)),
             pltpu.SemaphoreType.DMA((8, chunks)),
+            pltpu.SemaphoreType.DMA((tc, chunks)),
             pltpu.SemaphoreType.DMA((tc, chunks)),
             pltpu.SemaphoreType.DMA((tc, chunks)),
         ],
@@ -284,7 +349,7 @@
     small = vmem_plan(activations, cotangent, dp, tr, tc) < VMEM_BYTES * 3 // 4
     if dp == 4 and tr == 2 and tc > 2 and small:
         grad = gathered(activations, cotangent, dp, tr, tc)
-        grad = (grad.astype(jnp.float32) * (1.0 / SCALE)).reshape(master.shape)
+        grad = grad.reshape(master.shape)
     else:
         grad = native(activations, cotangent)
     new_moment = first_decay * moment + (1.0 - first_decay) * grad

time: 137 us -> 110 us (0.80)
  Pallas kernels: 129 us -> 101 us
    pallas_call x1, Pallas kernels: 129 us -> 101 us  [gathered(): pl.pallas_call(functools.partial(grad_kernel, (dp, tr, tc, chunks, tile))...]
where the time goes in v2:
time: 110 us; the launch traced here: 109 us
  Pallas kernels  101 us (92%)
  other arithmetic  6.92 us (6%)
    pallas_call x1, Pallas kernels, gathered(): pl.pallas_call(functools.partial(grad_kernel, (dp, tr, tc, chunks, tile))...  101 us
    sub x1, other arithmetic, shards(): new_master = master - learn_rate * (update + weight_decay * master)  6.92 us

profile of v2, /device:TPU:0, one launch (start us, length us, event | category | flops | bytes accessed | tf_op | source)
XLA Modules:
  0.0 108.7 jit_solution(9713319923065518293)
XLA Ops:
  0.6 0.0 copy-start
  0.6 101.2 %shard_map.76 = f32[96,8192]{1,0:T(8,128)} custom-call(bf16[256,1536]{1,0:T(8,128)(2,1)} %act.1, bf16[512,2048]{1,0:T(8,128)(2,1)} %cot.1), custom_call_target="tpu_custom_call" | custom-call | tf_op jit(solution)/shard_map/pallas_call | solution.py:298
  101.8 0.0 copy-done
  101.8 6.9 %multiply_subtract_fusion = (f32[1,96,8192]{2,1,0:T(8,128)}, f32[1,96,8192]{2,1,0:T(8,128)}, f32[1,96,8192]{2,1,0:T(8,128)}) fusion(f32[1,96,8192]{2,1,0:T(8,128)S(1)} %copy-done, f32[96,8192]{1,0:T(8,128)} %shard_map.76, f32[1,96,8192]{2,1,0:T(8,128)} %param.8, f32[1,96,8192]{2,1,0:T(8,128)} %param.9), kind=kLoop, calls=%fused_computation.4 | loop fusion | flops 11796480 | bytes 22020096 | tf_op jit(solution)/shard_map/sub | solution.py:358
Async XLA Ops:
  0.6 101.2 %copy-start = (f32[1,96,8192]{2,1,0:T(8,128)S(1)}, f32[1,96,8192]{2,1,0:T(8,128)}, u32[]{:S(2)}) copy-start(f32[1,96,8192]{2,1,0:T(8,128)} %param.7) | copy-start | bytes 9437188

commit v3 on v2

--- a/solution.py
+++ b/solution.py
@@ -16,8 +16,9 @@
 second_fix = 1.0 - 0.95**10
 
 MESH = pl.DeviceIdType.MESH
-VMEM_BYTES = 60 * 2**20
-CHUNKS = 4
+VMEM_BYTES = 40 * 2**20
+CHUNKS = 8
+AHEAD = 2
 LEVELS = 12.0
 STEPS = 128.0 * LEVELS
 
@@ -209,8 +210,8 @@
     for k in range(1, 4):
         a_dp(k).start()
     send_z(0, 0)
-    own(0)
-    own(1)
+    for u in range(AHEAD):
+        own(u)
     local_a.start()
     for u in range(chunks):
         local_c(u).start()
@@ -224,8 +225,8 @@
 
     def step_xy(u):
         got_xy(u)
-        if u + 2 < chunks:
-            own(u + 2)
+        if u + AHEAD < chunks:
+            own(u + AHEAD)
 
     def last_a(k):
         got_z(tc - 2, k)
@@ -233,34 +234,20 @@
             local_a.wait()
         at[rel[k]] = abuf[rel[k]].reshape(tc * atok, rows).T
 
-    moves = [(forward, s, k) for s in range(1, tc - 1) for k in range(4)]
-    moves += [(last_a, k) for k in range(4)]
-    turns = []
+    beat, turn = 4.4, 70.0 / chunks
+    tasks = []
+    for i in range(4 * (tc - 1)):
+        s, k = i // 4 + 1, i % 4
+        tasks.append((9 + beat * i, forward, (s, k)) if s < tc - 1 else (9 + beat * i, last_a, (k,)))
+    ready = 9 + beat * 4 * (tc - 1)
     for u in range(chunks):
-        turns.append((step_xy, u))
-        if u >= 1:
-            turns.append((got_diag, u - 1))
-    order = []
-    early = 2 * (chunks // 2)
-    for i, move in enumerate(moves):
-        order.append(move)
-        if i >= 2 and turns and (i - 2) % (len(moves) // early) == 0 and len(turns) > chunks // 2:
-            order.append(turns.pop(0))
-    for f, *args in order:
-        f(*args)
-    done = 0
-    for f, u in turns:
-        f(u)
-        if f is got_diag:
-            while done <= u:
-                compute(done)
-                done += 1
-    got_diag(chunks - 1)
-    while done < chunks:
-        compute(done)
-        done += 1
-    for u in range(chunks):
-        finish(u)
+        seen = 9 + turn * (u + 0.67)
+        tasks.append((seen, step_xy, (u,)))
+        tasks.append((seen + turn, got_diag, (u,)))
+        tasks.append((max(seen + turn, ready) + 0.1, compute, (u,)))
+        tasks.append((max(ready + (u + 1) * 35.0 / chunks, seen + turn) + 6, finish, (u,)))
+    for _, task, args in sorted(tasks, key=lambda entry: entry[0]):
+        task(*args)
 
     for k in range(1, 4):
         a_dp(k).wait_send()
@@ -298,7 +285,7 @@
     return pl.pallas_call(
         functools.partial(grad_kernel, (dp, tr, tc, chunks, tile)),
         out_shape=jax.ShapeDtypeStruct((owned, tc * units), jnp.float32),
-        in_specs=[pl.BlockSpec(memory_space=pl.ANY)] * 2,
+        in_specs=[pl.BlockSpec(memory_space=pltpu.HBM)] * 2,
         out_specs=pl.BlockSpec(memory_space=pl.ANY),
         scratch_shapes=[
             pltpu.VMEM((dp, tc, atok, rows), jnp.bfloat16),
@@ -346,7 +333,7 @@
 
 def shards(activations, cotangent, master, moment, second):
     dp, tr, tc = (lax.axis_size(name) for name in ("dp", "tr", "tc"))
-    small = vmem_plan(activations, cotangent, dp, tr, tc) < VMEM_BYTES * 3 // 4
+    small = vmem_plan(activations, cotangent, dp, tr, tc) < VMEM_BYTES * 7 // 8
     if dp == 4 and tr == 2 and tc > 2 and small:
         grad = gathered(activations, cotangent, dp, tr, tc)
         grad = grad.reshape(master.shape)

time: 110 us -> 113 us (1.027)
  local copies, waits for them, and re-layouts: 0.01 us -> 2.72 us
  Pallas kernels: 101 us -> 103 us
    unnamed x2 -> x6, local copies, waits for them, and re-layouts: 0.01 us -> 2.72 us
    pallas_call x1, Pallas kernels: 101 us -> 103 us  [gathered(): pl.pallas_call(functools.partial(grad_kernel, (dp, tr, tc, chunks, tile))...]
where the time goes in v3:
time: 113 us
  Pallas kernels  103 us (91%)
  other arithmetic  6.29 us (6%)
  local copies, waits for them, and re-layouts  2.72 us (2%)
    pallas_call x1, Pallas kernels, gathered(): pl.pallas_call(functools.partial(grad_kernel, (dp, tr, tc, chunks, tile))...  103 us
    sub x1, other arithmetic, shards(): new_master = master - learn_rate * (update + weight_decay * master)  6.29 us
    unnamed x6, local copies, waits for them, and re-layouts  2.72 us

profile of v3, /device:TPU:0, one launch (start us, length us, event | category | flops | bytes accessed | tf_op | source)
XLA Modules:
  0.0 112.8 jit_solution(6985999114560951128)
XLA Ops:
  0.6 0.0 copy-start
  0.6 1.6 %copy-done = bf16[512,2048]{1,0:T(8,128)(2,1)S(1)} copy-done((bf16[512,2048]{1,0:T(8,128)(2,1)S(1)}, bf16[512,2048]{1,0:T(8,128)(2,1)}, u32[]{:S(2)}) %copy-start) | copy-done | bytes 2097176
  2.2 0.0 copy-start.1
  2.2 1.1 %copy-done.1 = bf16[256,1536]{1,0:T(8,128)(2,1)S(1)} copy-done((bf16[256,1536]{1,0:T(8,128)(2,1)S(1)}, bf16[256,1536]{1,0:T(8,128)(2,1)}, u32[]{:S(2)}) %copy-start.1) | copy-done | bytes 786456
  3.4 0.0 copy-start.2
  3.4 103.1 %shard_map.76 = f32[96,8192]{1,0:T(8,128)S(1)} custom-call(bf16[256,1536]{1,0:T(8,128)(2,1)S(1)} %copy-done.1, bf16[512,2048]{1,0:T(8,128)(2,1)S(1)} %copy-done), custom_call_target="tpu_custom_call" | custom-call | tf_op jit(solution)/shard_map/pallas_call | solution.py:285
  106.5 0.0 copy-done.2
  106.5 6.3 %multiply_subtract_fusion = (f32[1,96,8192]{2,1,0:T(8,128)}, f32[1,96,8192]{2,1,0:T(8,128)}, f32[1,96,8192]{2,1,0:T(8,128)}) fusion(f32[1,96,8192]{2,1,0:T(8,128)S(1)} %copy-done.2, f32[96,8192]{1,0:T(8,128)S(1)} %shard_map.76, f32[1,96,8192]{2,1,0:T(8,128)} %param.8, f32[1,96,8192]{2,1,0:T(8,128)} %param.9), kind=kLoop, calls=%fused_computation.4 | loop fusion | flops 11796480 | bytes 22020096 | tf_op jit(solution)/shard_map/sub | solution.py:345
Async XLA Ops:
  0.6 1.6 %copy-start = (bf16[512,2048]{1,0:T(8,128)(2,1)S(1)}, bf16[512,2048]{1,0:T(8,128)(2,1)}, u32[]{:S(2)}) copy-start(bf16[512,2048]{1,0:T(8,128)(2,1)} %cot.1) | copy-start | bytes 6291460
  2.2 1.1 %copy-start.1 = (bf16[256,1536]{1,0:T(8,128)(2,1)S(1)}, bf16[256,1536]{1,0:T(8,128)(2,1)}, u32[]{:S(2)}) copy-start(bf16[256,1536]{1,0:T(8,128)(2,1)} %act.1) | copy-start | bytes 2359300
  3.4 103.1 %copy-start.2 = (f32[1,96,8192]{2,1,0:T(8,128)S(1)}, f32[1,96,8192]{2,1,0:T(8,128)}, u32[]{:S(2)}) copy-start(f32[1,96,8192]{2,1,0:T(8,128)} %param.7) | copy-start | bytes 9437188

commit v4 on v3

--- a/solution.py
+++ b/solution.py
@@ -16,9 +16,10 @@
 second_fix = 1.0 - 0.95**10
 
 MESH = pl.DeviceIdType.MESH
-VMEM_BYTES = 40 * 2**20
+VMEM_BYTES = 60 * 2**20
 CHUNKS = 8
 AHEAD = 2
+EARLY = 2
 LEVELS = 12.0
 STEPS = 128.0 * LEVELS
 
@@ -65,7 +66,7 @@
     return jnp.where(code < 0.0, -y, y)
 
 
-def grad_kernel(sizes, act, cot, out, abuf, cbuf, at, obuf, rbuf, dbuf, ld_sem, adp_s, adp_r, az_s, az_r, c_s, c_r, o_s, o_r, st_sem):
+def grad_kernel(sizes, act, cot, out, abuf, cbuf, at, obuf, rbuf, dbuf, sums, ld_sem, adp_s, adp_r, az_s, az_r, c_s, c_r, o_s, o_r, st_sem):
     dp, tr, tc, chunks, tile = sizes
     r, c, z = lax.axis_index("dp"), lax.axis_index("tr"), lax.axis_index("tc")
     rx = r + 1 - 2 * lax.rem(r, 2)
@@ -171,18 +172,36 @@
 
     owned = rows // tc
 
-    def compute(u):
-        for flow in range(4, 8):
-            c_copy(flow, u).wait_recv()
-        local_c(u).wait()
+    def product(q, u, cols):
+        rhs = cbuf[u, q, :, :, cols].reshape(tr * ctok, tile)
+        return jnp.dot(at[q], rhs, preferred_element_type=jnp.float32)
+
+    def partial(k, u):
+        c_copy(4 + k, u).wait_recv()
+        if k == 0:
+            local_c(u).wait()
 
         @pl.loop(0, nu // tile)
         def _(t):
             cols = pl.ds(pl.multiple_of(t * tile, tile), tile)
-            total = jnp.zeros((rows, tile), jnp.float32)
-            for q in range(dp):
-                rhs = cbuf[u, q, :, :, cols].reshape(tr * ctok, tile)
-                total += jnp.dot(at[q], rhs, preferred_element_type=jnp.float32)
+            term = product(rel[k], u, cols)
+            sums[u, :, cols] = term if k == 0 else sums[u, :, cols] + term
+
+    def compute(u):
+        for flow in range(7 if u < EARLY else 4, 8):
+            c_copy(flow, u).wait_recv()
+        if u >= EARLY:
+            local_c(u).wait()
+
+        @pl.loop(0, nu // tile)
+        def _(t):
+            cols = pl.ds(pl.multiple_of(t * tile, tile), tile)
+            if u < EARLY:
+                total = sums[u, :, cols] + product(rel[3], u, cols)
+            else:
+                total = jnp.zeros((rows, tile), jnp.float32)
+                for q in range(dp):
+                    total += product(q, u, cols)
             for j in range(tc):
                 part = total[j * owned:(j + 1) * owned]
                 obuf[u, j, :, cols] = encode(part)
@@ -191,7 +210,7 @@
                 def _():
                     dbuf[u, j, :, cols] = part
 
-        for j in range(1, tc):
+        for j in (2, 1, *range(3, tc)):
             o_copy(j, u).start()
         store(z, 0, u).start()
 
@@ -233,6 +252,9 @@
         if k == 0:
             local_a.wait()
         at[rel[k]] = abuf[rel[k]].reshape(tc * atok, rows).T
+        if k < 3:
+            for u in range(EARLY):
+                partial(k, u)
 
     beat, turn = 4.4, 70.0 / chunks
     tasks = []
@@ -294,6 +316,7 @@
             pltpu.VMEM((chunks, tc, owned, nu), jnp.bfloat16),
             pltpu.VMEM((chunks, tc, owned, nu), jnp.bfloat16),
             pltpu.VMEM((chunks, tc, owned, nu), jnp.float32),
+            pltpu.VMEM((EARLY, rows, nu), jnp.float32),
             pltpu.SemaphoreType.DMA((1 + chunks,)),
             pltpu.SemaphoreType.DMA((4,)),
             pltpu.SemaphoreType.DMA((4,)),
@@ -333,7 +356,7 @@
 
 def shards(activations, cotangent, master, moment, second):
     dp, tr, tc = (lax.axis_size(name) for name in ("dp", "tr", "tc"))
-    small = vmem_plan(activations, cotangent, dp, tr, tc) < VMEM_BYTES * 7 // 8
+    small = vmem_plan(activations, cotangent, dp, tr, tc) < VMEM_BYTES * 3 // 4
     if dp == 4 and tr == 2 and tc > 2 and small:
         grad = gathered(activations, cotangent, dp, tr, tc)
         grad = grad.reshape(master.shape)

time: 113 us -> 110 us (0.973)
  local copies, waits for them, and re-layouts: 2.72 us -> 0.01 us
    unnamed x6 -> x2, local copies, waits for them, and re-layouts: 2.72 us -> 0.01 us
where the time goes in v4:
time: 110 us
  Pallas kernels  102 us (93%)
  other arithmetic  6.92 us (6%)
    pallas_call x1, Pallas kernels, gathered(): pl.pallas_call(functools.partial(grad_kernel, (dp, tr, tc, chunks, tile))...  102 us
    sub x1, other arithmetic, shards(): new_master = master - learn_rate * (update + weight_decay * master)  6.92 us

profile of v4, /device:TPU:0, one launch (start us, length us, event | category | flops | bytes accessed | tf_op | source)
XLA Modules:
  0.0 109.7 jit_solution(13906593289642238707)
XLA Ops:
  0.6 0.0 copy-start
  0.6 102.1 %shard_map.76 = f32[96,8192]{1,0:T(8,128)} custom-call(bf16[256,1536]{1,0:T(8,128)(2,1)} %act.1, bf16[512,2048]{1,0:T(8,128)(2,1)} %cot.1), custom_call_target="tpu_custom_call" | custom-call | tf_op jit(solution)/shard_map/pallas_call | solution.py:307
  102.8 0.0 copy-done
  102.8 6.9 %multiply_subtract_fusion = (f32[1,96,8192]{2,1,0:T(8,128)}, f32[1,96,8192]{2,1,0:T(8,128)}, f32[1,96,8192]{2,1,0:T(8,128)}) fusion(f32[1,96,8192]{2,1,0:T(8,128)S(1)} %copy-done, f32[96,8192]{1,0:T(8,128)} %shard_map.76, f32[1,96,8192]{2,1,0:T(8,128)} %param.8, f32[1,96,8192]{2,1,0:T(8,128)} %param.9), kind=kLoop, calls=%fused_computation.4 | loop fusion | flops 11796480 | bytes 22020096 | tf_op jit(solution)/shard_map/sub | solution.py:368
Async XLA Ops:
  0.6 102.1 %copy-start = (f32[1,96,8192]{2,1,0:T(8,128)S(1)}, f32[1,96,8192]{2,1,0:T(8,128)}, u32[]{:S(2)}) copy-start(f32[1,96,8192]{2,1,0:T(8,128)} %param.7) | copy-start | bytes 9437188
